TPU v7x, 128 devices: a whole 4x4x4 slice. The times are simulated.
128 devices in a mesh: user: 16 (over y, z), item: 8 (over x, core).
Axes of the slice: x: 4, y: 4, z: 4, core: 2. Of those that a mesh axis runs over, the one named last changes fastest.
Arguments:
- tile_values: bfloat16 [256, 32, 256, 128], P('user', 'item'), may hold values from -600 to 600
- tile_ids: int32 [256, 32], P('user', 'item'), may hold values from 0 to 2047, as said below
- lengths: int32 [256], P('user'), may hold values from 128 to 256
- user_weights: float32 [256, 256], P('user'), may hold values from 0.5 to 16
- time_factor: float32 [256, 256], replicated, may hold values from -0.25 to 2.25
- item_factor: bfloat16 [262144, 256], P(('item', 'user')), may hold values from -0.2421875 to 0.2421875
Outputs:
- slices: bfloat16 [256, 256, 256], P(('user', 'item'))
- new_time: float32 [256, 256], replicated
- new_items: float32 [262144, 256], P(('item', 'user'))
Inputs may be any that keep to these rules, and one draw needn't show every extreme that they name: `tile_ids`: slot block i of a user (slots i * 4 to (i + 1) * 4 - 1) names tiles i * 256 to (i + 1) * 256 - 1. Within the slots of 16 users of one index of user in one slot block, all tiles differ, and at most 8 of them lie in one group of 16 tiles (group g: tiles i * 256 + g * 16 onward); in every slot block some group holds exactly 8 of them for every index of user.
All inputs are finite; a program needn't handle non-finite values.
Results may differ from a plain program's by a relative error of at most 0.014.
Values may be sent and summed in bfloat16 or wider, within the bound.
A program may use at most 128 MiB of HBM per device.

v0:
```python
import jax
import jax.numpy as jnp
from jax import lax
from jax.sharding import PartitionSpec as P

NS_STEPS = 6
HIGHEST = lax.Precision.HIGHEST
EPSILON = 1e-06


def polar_batch(target):
    norm_scale = jnp.sqrt(jnp.sum(target * target, axis=(1, 2), keepdims=True) + EPSILON)
    iterate = target / norm_scale
    for _ in range(NS_STEPS):
        gram = jnp.einsum("krc,krd->kcd", iterate, iterate, precision=HIGHEST)
        iterate = 1.5 * iterate - 0.5 * jnp.einsum("krc,kcd->krd", iterate, gram, precision=HIGHEST)
    return iterate


def spd_solve(gram_matrix, right_side):
    chol_lower = jnp.linalg.cholesky(gram_matrix)
    return jax.scipy.linalg.cho_solve((chol_lower, True), right_side.T).T


def body(tile_values, tile_ids, lengths, user_weights, time_factor, item_factor):
    user_count = lax.axis_size("user")
    item_count = lax.axis_size("item")
    item_pos = lax.axis_index("item")
    users_here, slots_user, time_rows, tile_width = tile_values.shape
    rank_size = time_factor.shape[0]
    tiles_owned = item_factor.shape[0] // tile_width
    slot_count = users_here * slots_user
    share_count = users_here // item_count
    flat_ids = (tile_ids - item_pos * (tiles_owned * user_count)).reshape(slot_count)
    live = jnp.arange(time_rows, dtype=jnp.int32)[None, :] < lengths[:, None]
    shard_rows = lax.all_gather(item_factor, "user", axis=0, tiled=True)
    panels = shard_rows.reshape(tiles_owned * user_count, tile_width, rank_size)[flat_ids]
    panels = panels.reshape(users_here, slots_user, tile_width, rank_size)
    partial = jnp.einsum("ksrt,kstc->krc", tile_values, panels, preferred_element_type=jnp.float32)
    partial = jnp.where(live[:, :, None], partial, 0.0)
    share_start = item_pos * share_count
    share_weights = lax.dynamic_slice_in_dim(user_weights, share_start, share_count, 0)
    projection = lax.psum_scatter(partial, "item", scatter_dimension=0, tiled=True)
    scaled = projection * share_weights[:, None, :]
    polar = polar_batch(jnp.einsum("krc,dc->krd", scaled, time_factor, precision=HIGHEST))
    slices = polar.astype(jnp.bfloat16)
    time_term = jnp.einsum("krc,krd->cd", polar, scaled, precision=HIGHEST)
    weight_term = jnp.dot(share_weights.T, share_weights, precision=HIGHEST)
    item_term = jnp.dot(item_factor.T, item_factor, preferred_element_type=jnp.float32)
    sums = lax.psum((time_term, weight_term, item_term), "item")
    time_mttkrp, weight_gram, item_inner = lax.psum(sums, "user")
    polar_all = lax.all_gather(slices, "item", axis=0, tiled=True).astype(jnp.float32)
    time_raw = spd_solve(item_inner * weight_gram, time_mttkrp)
    new_time = time_raw / jnp.sqrt(jnp.sum(time_raw * time_raw, axis=0, keepdims=True) + EPSILON)
    item_gram = jnp.dot(new_time.T, new_time, precision=HIGHEST) * weight_gram
    user_maps = (
        jnp.einsum("krc,cd->krd", polar_all, new_time, precision=HIGHEST) * user_weights[:, None, :]
    )
    user_maps = jnp.where(live[:, :, None], user_maps, 0.0).astype(jnp.bfloat16)
    tile_terms = jnp.einsum(
        "ksrt,krc->kstc", tile_values, user_maps, preferred_element_type=jnp.float32
    ).astype(jnp.bfloat16)
    tile_terms = tile_terms.reshape(slot_count, tile_width * rank_size)
    row_count = tiles_owned * tile_width * user_count
    wanted = jnp.arange(row_count // tile_width, dtype=jnp.int32)
    hits = (flat_ids[None, :] == wanted[:, None]).astype(jnp.bfloat16)
    summed = jnp.dot(hits, tile_terms, preferred_element_type=jnp.float32)
    item_mttkrp = lax.psum_scatter(
        summed.reshape(row_count, rank_size).astype(jnp.bfloat16),
        "user",
        scatter_dimension=0,
        tiled=True,
    ).astype(jnp.float32)
    new_items = spd_solve(item_gram, item_mttkrp)
    return (slices, new_time, new_items)


def solution(mesh):
    in_specs = (
        P("user", "item", None, None),
        P("user", "item"),
        P("user"),
        P("user", None),
        P(),
        P(("item", "user"), None),
    )
    out_specs = (P(("user", "item"), None, None), P(), P(("item", "user"), None))
    return jax.shard_map(body, mesh=mesh, in_specs=in_specs, out_specs=out_specs, check_vma=False)
```

profile of v0, /device:TPU:1, one launch (start us, length us, event | category | flops | bytes accessed | tf_op | source)
XLA Modules:
  0.0 606.0 jit_solution(13550863670987385643)
XLA Ops:
  8.9 0.7 iota_compare_fusion.5
  9.6 114.9 %all-gather.3.cloned.1.call-done = bf16[32768,256]{1,0:T(8,128)(2,1)} async-done(((bf16[2048,256]{1,0:T(8,128)(2,1)}), bf16[32768,256]{1,0:T(8,128)(2,1)}) %all-gather.3.cloned.1.call-update) | async-done | bytes 16777232 | tf_op jit(solution)/shard_map/all_gather | solution.py:36
  124.5 8.5 %gather_fusion = bf16[64,128,256]{2,1,0:T(8,128)(2,1)} fusion(bf16[256,128,256]{2,1,0:T(8,128)(2,1)} %bitcast.145, s32[1024]{0:T(1024)S(1)} %pad_clamp_fusion), kind=kCustom, calls=%fused_computation | custom fusion | bytes 8388864 | tf_op jit(solution)/shard_map/gather | solution.py:37
  133.0 6.7 %fusion = f32[16,256,256]{1,2,0:T(8,128)} fusion(bf16[16,4,128,256]{3,2,1,0:T(8,128)(2,1)} %bitcast.142, bf16[16,4,256,128]{3,2,1,0:T(8,128)(2,1)} %param.7, pred[16,256]{1,0:T(8,128)(4,1)S(1)} %iota_compare_fusion.5), kind=kOutput, calls=%fused_computation.7 | convolution fusion | flops 1074790400 | bytes 12587008 | tf_op jit(solution)/shard_map/ksrt,kstc->krc/dot_general | solution.py:39
  140.5 1.1 fusion.53
  141.7 1.2 fusion.52
  142.9 31.8 %reduce-scatter.3.cloned.1.call-done = f32[2,256,256]{1,2,0:T(8,128)} async-done(((f32[16,256,256]{1,2,0:T(8,128)}), f32[2,256,256]{1,2,0:T(8,128)}) %reduce-scatter.3.cloned.1.call-update) | async-done | bytes 524304 | tf_op jit(solution)/shard_map/reduce_scatter | solution.py:43
  174.7 2.2 multiply_reduce_fusion
  176.9 1.2 fusion.22
  178.8 1.1 fusion.47
  180.5 1.1 fusion.48
  182.3 1.1 fusion.49
  184.1 1.1 fusion.50
  185.8 1.1 fusion.51
  186.9 1.4 fusion.46
  188.3 2.0 convolution_bitcast_fusion
  190.3 61.9 %all-reduce.8.cloned.1.call-done = (f32[256,256]{1,0:T(8,128)}, f32[256,256]{0,1:T(8,128)}, f32[256,256]{0,1:T(8,128)}) async-done(((f32[256,256]{1,0:T(8,128)}, f32[256,256]{0,1:T(8,128)}, f32[256,256]{0,1:T(8,128)}), (f32[256,256]{1,0:T(8,128)}, f32[256,256]{0,1:T(8,128)}, f32[256,256]{0,1:T(8,128)})) %all-reduce.8.cloned.1.call-update) | async-done | bytes 786448 | tf_op jit(solution)/shard_map/psum | solution.py:50
  252.8 89.9 %all-reduce.6.cloned.1.call-done = (f32[256,256]{0,1:T(8,128)}, f32[256,256]{0,1:T(8,128)}, f32[256,256]{0,1:T(8,128)}) async-done(((f32[256,256]{0,1:T(8,128)}, f32[256,256]{0,1:T(8,128)}, f32[256,256]{0,1:T(8,128)}), (f32[256,256]{0,1:T(8,128)}, f32[256,256]{0,1:T(8,128)}, f32[256,256]{0,1:T(8,128)})) %all-reduce.6.cloned.1.call-update) | async-done | bytes 786448 | tf_op jit(solution)/shard_map/psum | solution.py:51
  342.7 1.1 mul.88
  344.0 11.7 %cholesky.130 = f32[128,128]{1,0:T(8,128)S(1)} custom-call(f32[128,128]{1,0:T(8,128)S(1)} %cholesky.194), custom_call_target="Cholesky" | custom-call | tf_op jit(solution)/shard_map/jit(cholesky)/cholesky | solution.py:21
  355.8 9.8 %custom-call.25 = f32[1,128,128]{1,2,0:T(8,128)S(1)} custom-call(f32[1,128,128]{2,1,0:T(8,128)S(1)} %get-tuple-element.62), custom_call_target="InvertDiagBlocksLowerTriangular" | custom-call | tf_op jit(solution)/shard_map/jit(cholesky)/cholesky | solution.py:21
  366.1 11.7 %cholesky.147 = f32[128,128]{1,0:T(8,128)S(1)} custom-call(f32[128,128]{1,0:T(8,128)S(1)} %convolution_subtract_fusion.5), custom_call_target="Cholesky" | custom-call | tf_op jit(solution)/shard_map/jit(cholesky)/cholesky | solution.py:21
  380.0 4.3 while.2
  380.9 1.4 bitcast_dynamic-update-slice_fusion.4
  382.9 1.4 bitcast_dynamic-update-slice_fusion.4
  384.4 19.7 %custom-call.22 = f32[2,128,128]{1,2,0:T(8,128)S(1)} custom-call(f32[2,128,128]{2,1,0:T(8,128)S(1)} %get-tuple-element.11), custom_call_target="InvertDiagBlocksLowerTriangular" | custom-call | tf_op jit(solution)/shard_map/jit(_cho_solve)/triangular_solve | solution.py:22
  406.1 3.6 select_convert_fusion
  409.8 3.2 convert_bitcast_fusion
  413.0 6.8 %copy.78 = bf16[8,8,128,256]{3,1,2,0:T(8,128)(2,1)} copy(bf16[8,8,128,256]{2,3,1,0:T(8,128)(2,1)} %bitcast.143) | data formatting | bytes 8388608
  419.8 10.2 %convolution_convert_fusion = bf16[256,32768]{1,0:T(8,128)(2,1)} fusion(bf16[64,32768]{1,0:T(8,128)(2,1)} %bitcast.144, s32[64]{0:T(128)S(1)} %eq.15), kind=kOutput, calls=%fused_computation.5 | convolution fusion | flops 1082146816 | bytes 20971776 | tf_op jit(solution)/shard_map/dot_general | solution.py:67
  430.0 25.6 %convert_element_type.26 = bf16[32768,256]{1,0:T(8,128)(2,1)} reshape(bf16[256,32768]{1,0:T(8,128)(2,1)} %convolution_convert_fusion) | data formatting | bytes 33554432 | tf_op jit(solution)/shard_map/convert_element_type | solution.py:69
  455.6 21.6 %copy.58 = bf16[32768,256]{0,1:T(8,128)(2,1)} copy(bf16[32768,256]{1,0:T(8,128)(2,1)} %convert_element_type.26) | data formatting | bytes 33554432 | tf_op jit(solution)/shard_map/convert_element_type | solution.py:69
  477.4 0.8 copy.59
  478.9 11.7 %cholesky.164 = f32[128,128]{1,0:T(8,128)S(1)} custom-call(f32[128,128]{1,0:T(8,128)S(1)} %cholesky.197), custom_call_target="Cholesky" | custom-call | tf_op jit(solution)/shard_map/jit(cholesky)/cholesky | solution.py:21
  490.7 9.8 %custom-call.26 = f32[1,128,128]{1,2,0:T(8,128)S(1)} custom-call(f32[1,128,128]{2,1,0:T(8,128)S(1)} %get-tuple-element.58), custom_call_target="InvertDiagBlocksLowerTriangular" | custom-call | tf_op jit(solution)/shard_map/jit(cholesky)/cholesky | solution.py:21
  501.0 11.7 %cholesky.181 = f32[128,128]{1,0:T(8,128)S(1)} custom-call(f32[128,128]{1,0:T(8,128)S(1)} %convolution_subtract_fusion.4), custom_call_target="Cholesky" | custom-call | tf_op jit(solution)/shard_map/jit(cholesky)/cholesky | solution.py:21
  515.4 4.0 while.3
  516.0 1.4 bitcast_dynamic-update-slice_fusion.5
  518.0 1.4 bitcast_dynamic-update-slice_fusion.5
  519.4 19.8 %custom-call.23 = f32[2,128,128]{1,2,0:T(8,128)S(1)} custom-call(f32[2,128,128]{2,1,0:T(8,128)S(1)} %get-tuple-element.19), custom_call_target="InvertDiagBlocksLowerTriangular" | custom-call | tf_op jit(solution)/shard_map/jit(_cho_solve)/triangular_solve | solution.py:22
  539.2 49.8 %reduce-scatter.5.cloned.1.call-done = bf16[2048,256]{0,1:T(8,128)(2,1)} async-done(((bf16[32768,256]{0,1:T(8,128)(2,1)}), bf16[2048,256]{0,1:T(8,128)(2,1)}) %reduce-scatter.5.cloned.1.call-update) | async-done | bytes 1048592 | tf_op jit(solution)/shard_map/reduce_scatter | solution.py:68
  589.1 1.7 fusion.8
  590.7 2.1 convolution_subtract_fusion.1
  592.8 1.1 fusion.35
  593.9 1.0 fusion.34
  594.9 1.0 convolution_subtract_fusion
  595.9 1.0 fusion.33
  597.1 1.8 copy.60
  (86 shorter events, 15.3 us)
Async XLA Ops:
  7.2 167.5 %copy-start = (f32[256,256]{1,0:T(8,128)S(1)}, f32[256,256]{1,0:T(8,128)}, u32[]{:S(2)}) copy-start(f32[256,256]{1,0:T(8,128)} %param.11) | copy-start | bytes 786436
  7.2 117.4 %all-gather.3.cloned.1.call-start = ((), (), s32[]{:S(2)}) async-start(), calls=%async_computation.2 | async-start | bytes 17825792 | tf_op jit(solution)/shard_map/all_gather | solution.py:36
  7.9 166.8 %reduce-scatter.3.cloned.1.call-start = ((), (), s32[]{:S(2)}) async-start(), calls=%async_computation.3 | async-start | bytes 4718592 | tf_op jit(solution)/shard_map/reduce_scatter | solution.py:43
  139.8 0.7 copy-start.7
  139.8 1.9 copy-start.4
  139.8 112.4 %all-reduce.8.cloned.1.call-start = ((), (), s32[]{:S(2)}) async-start(), calls=%async_computation.7 | async-start | bytes 1572864 | tf_op jit(solution)/shard_map/psum | solution.py:50
  183.4 4.9 copy-start.3
  190.3 152.5 %all-reduce.6.cloned.1.call-start = ((), (), s32[]{:S(2)}) async-start(), calls=%async_computation.6 | async-start | bytes 1572864 | tf_op jit(solution)/shard_map/psum | solution.py:51
  252.2 153.9 %all-gather.5.cloned.1.call-start = ((), (), s32[]{:S(2)}) async-start(), calls=%async_computation.4 | async-start | bytes 2359296 | tf_op jit(solution)/shard_map/all_gather | solution.py:52
  252.8 336.3 %reduce-scatter.5.cloned.1.call-start = ((), (), s32[]{:S(2)}) async-start(), calls=%async_computation.5 | async-start | bytes 17825792 | tf_op jit(solution)/shard_map/reduce_scatter | solution.py:68
  342.7 61.3 %copy-start.6 = (f32[256,256]{0,1:T(8,128)S(1)}, f32[256,256]{0,1:T(8,128)}, u32[]{:S(2)}) copy-start(f32[256,256]{0,1:T(8,128)} %get-tuple-element.45) | copy-start | bytes 786436
  406.1 3.7 copy-start.2
  477.3 1.0 copy-start.5
  595.9 3.0 copy-start.1
Sparse Core Ops, SparseCore 0:
  10.1 114.3 all-gather.2
  139.9 34.6 reduce-scatter.2
  190.4 61.7 all-reduce.7
  255.6 87.0 all-reduce.5
  344.9 26.7 all-gather.4
  477.4 111.6 reduce-scatter.4
where the time goes:
time: 618 us; the launch traced here: 606 us
  waiting for transfers between devices  350 us (57%)
  other arithmetic  111 us (18%)
  local copies, waits for them, and re-layouts  74.5 us (12%)
  matrix products  52.8 us (9%)
  between operations  17.4 us (3%)
    all_gather x1, waiting for transfers between devices, body(): shard_rows = lax.all_gather(item_factor, 'user', axis=0, tiled=True)  115 us
    psum x1, waiting for transfers between devices, body(): time_mttkrp, weight_gram, item_inner = lax.psum(sums, 'user')  89.9 us
    another operation x13, other arithmetic, spd_solve(): chol_lower = jnp.linalg.cholesky(gram_matrix)  68.7 us
    psum x1, waiting for transfers between devices, body(): sums = lax.psum((time_term, weight_term, item_term), 'item')  61.9 us
    reduce_scatter x1, waiting for transfers between devices, body(): lax.psum_scatter(summed.reshape(row_count, rank_size).astype(jnp.bfloat16...  49.8 us
    convert_element_type x2, local copies, waits for them, and re-layouts, body(): summed.reshape(row_count, rank_size).astype(jnp.bfloat16)  47.3 us
    another operation x5, other arithmetic, spd_solve(): return jax.scipy.linalg.cho_solve((chol_lower, True), right_side.T).T  39.6 us
    reduce_scatter x1, waiting for transfers between devices, body(): lax.psum_scatter(partial, 'item', scatter_dimension=0, tiled=True)  31.8 us
  transfers between devices with their start and end apart: 6, of which 5 were waited for; matrix products, arithmetic and copies ran while one was open for 21% of the time, Pallas kernels for 0%

commit v1 on v0

--- a/solution.py
+++ b/solution.py
@@ -33,7 +33,9 @@
     share_count = users_here // item_count
     flat_ids = (tile_ids - item_pos * (tiles_owned * user_count)).reshape(slot_count)
     live = jnp.arange(time_rows, dtype=jnp.int32)[None, :] < lengths[:, None]
-    shard_rows = lax.all_gather(item_factor, "user", axis=0, tiled=True)
+    shard_rows = jnp.concatenate(
+        lax.all_to_all(jnp.stack([item_factor] * lax.axis_size("user")), "user", 0, 0), axis=0
+    )
     panels = shard_rows.reshape(tiles_owned * user_count, tile_width, rank_size)[flat_ids]
     panels = panels.reshape(users_here, slots_user, tile_width, rank_size)
     partial = jnp.einsum("ksrt,kstc->krc", tile_values, panels, preferred_element_type=jnp.float32)

time: 618 us -> 807 us (1.31); the launches traced: 606 us -> 803 us
  waiting for transfers between devices: 350 us -> 533 us
  starting transfers between devices: 0.24 us -> 9.5 us
    all_to_all x0 -> x1, waiting for transfers between devices: none -> 293 us  [body(): lax.all_to_all(jnp.stack([item_factor] * lax.axis_size('user')), 'user',...]
    all_gather x1 -> x0, waiting for transfers between devices: 115 us -> none  [body(): shard_rows = lax.all_gather(item_factor, 'user', axis=0, tiled=True)]
    all_to_all x0 -> x1, starting transfers between devices: none -> 8.77 us  [body(): lax.all_to_all(jnp.stack([item_factor] * lax.axis_size('user')), 'user',...]
  transfers between devices with their start and end apart: 6 -> 6, of which waited for: 5 -> 5; matrix products, arithmetic and copies ran while one was open for 21% -> 15% of each run, Pallas kernels for 0% -> 0%
where the time goes in v1:
time: 807 us; the launch traced here: 803 us
  waiting for transfers between devices  533 us (66%)
  other arithmetic  110 us (14%)
  local copies, waits for them, and re-layouts  80.6 us (10%)
  matrix products  52.8 us (7%)
  between operations  17 us (2%)
  starting transfers between devices  9.5 us (1%)
    all_to_all x1, waiting for transfers between devices, body(): lax.all_to_all(jnp.stack([item_factor] * lax.axis_size('user')), 'user',...  293 us
    psum x1, waiting for transfers between devices, body(): time_mttkrp, weight_gram, item_inner = lax.psum(sums, 'user')  90 us
    another operation x13, other arithmetic, spd_solve(): chol_lower = jnp.linalg.cholesky(gram_matrix)  68.6 us
    psum x1, waiting for transfers between devices, body(): sums = lax.psum((time_term, weight_term, item_term), 'item')  61.7 us
    reduce_scatter x1, waiting for transfers between devices, body(): lax.psum_scatter(summed.reshape(row_count, rank_size).astype(jnp.bfloat16...  50 us
    convert_element_type x2, local copies, waits for them, and re-layouts, body(): summed.reshape(row_count, rank_size).astype(jnp.bfloat16)  47.3 us
    another operation x5, other arithmetic, spd_solve(): return jax.scipy.linalg.cho_solve((chol_lower, True), right_side.T).T  39.6 us
    reduce_scatter x1, waiting for transfers between devices, body(): lax.psum_scatter(partial, 'item', scatter_dimension=0, tiled=True)  37.9 us
  transfers between devices with their start and end apart: 6, of which 5 were waited for; matrix products, arithmetic and copies ran while one was open for 15% of the time, Pallas kernels for 0%

profile of v1, /device:TPU:1, one launch (start us, length us, event | category | flops | bytes accessed | tf_op | source)
XLA Modules:
  0.0 803.1 jit_solution(8077666156026588031)
XLA Ops:
  7.2 6.9 stack.2
  14.0 8.8 %all-to-all-start = ((bf16[16,2048,256]{2,1,0:T(8,128)(2,1)}), bf16[16,2048,256]{2,1,0:T(8,128)(2,1)}, u32[]{:S(2)}, u32[]{:S(2)}) async-start(bf16[16,2048,256]{2,1,0:T(8,128)(2,1)} %stack.2), calls=%async_computation | async-start | bytes 33554432 | tf_op jit(solution)/shard_map/all_to_all | solution.py:37
  23.2 293.0 %all-to-all-done = bf16[16,2048,256]{2,1,0:T(8,128)(2,1)} async-done(((bf16[16,2048,256]{2,1,0:T(8,128)(2,1)}), bf16[16,2048,256]{2,1,0:T(8,128)(2,1)}, u32[]{:S(2)}, u32[]{:S(2)}) %all-to-all-start) | async-done | bytes 16777248 | tf_op jit(solution)/shard_map/all_to_all | solution.py:37
  316.1 8.5 %gather_fusion = bf16[64,128,256]{2,1,0:T(8,128)(2,1)} fusion(bf16[256,128,256]{2,1,0:T(8,128)(2,1)} %bitcast, s32[1024]{0:T(1024)S(1)} %pad_clamp_fusion), kind=kCustom, calls=%fused_computation | custom fusion | bytes 8388864 | tf_op jit(solution)/shard_map/gather | solution.py:39
  324.7 6.7 fusion
  332.1 1.1 fusion.53
  333.3 1.2 fusion.52
  334.5 37.9 %reduce-scatter.3.cloned.1.call-done = f32[2,256,256]{1,2,0:T(8,128)} async-done(((f32[16,256,256]{1,2,0:T(8,128)}), f32[2,256,256]{1,2,0:T(8,128)}) %reduce-scatter.3.cloned.1.call-update) | async-done | bytes 524304 | tf_op jit(solution)/shard_map/reduce_scatter | solution.py:45
  372.4 2.2 multiply_reduce_fusion
  374.6 1.2 fusion.22
  376.5 1.1 fusion.47
  378.3 1.1 fusion.48
  380.0 1.1 fusion.49
  381.8 1.1 fusion.50
  383.6 1.1 fusion.51
  384.6 1.4 fusion.46
  386.0 2.0 convolution_bitcast_fusion
  388.0 61.7 %all-reduce.8.cloned.1.call-done = (f32[256,256]{1,0:T(8,128)}, f32[256,256]{0,1:T(8,128)}, f32[256,256]{0,1:T(8,128)}) async-done(((f32[256,256]{1,0:T(8,128)}, f32[256,256]{0,1:T(8,128)}, f32[256,256]{0,1:T(8,128)}), (f32[256,256]{1,0:T(8,128)}, f32[256,256]{0,1:T(8,128)}, f32[256,256]{0,1:T(8,128)})) %all-reduce.8.cloned.1.call-update) | async-done | bytes 786448 | tf_op jit(solution)/shard_map/psum | solution.py:52
  450.4 90.0 %all-reduce.6.cloned.1.call-done = (f32[256,256]{0,1:T(8,128)}, f32[256,256]{0,1:T(8,128)}, f32[256,256]{0,1:T(8,128)}) async-done(((f32[256,256]{0,1:T(8,128)}, f32[256,256]{0,1:T(8,128)}, f32[256,256]{0,1:T(8,128)}), (f32[256,256]{0,1:T(8,128)}, f32[256,256]{0,1:T(8,128)}, f32[256,256]{0,1:T(8,128)})) %all-reduce.6.cloned.1.call-update) | async-done | bytes 786448 | tf_op jit(solution)/shard_map/psum | solution.py:53
  540.5 1.1 mul.88
  541.8 11.7 %cholesky.130 = f32[128,128]{1,0:T(8,128)S(1)} custom-call(f32[128,128]{1,0:T(8,128)S(1)} %cholesky.194), custom_call_target="Cholesky" | custom-call | tf_op jit(solution)/shard_map/jit(cholesky)/cholesky | solution.py:21
  553.5 9.8 %custom-call.25 = f32[1,128,128]{1,2,0:T(8,128)S(1)} custom-call(f32[1,128,128]{2,1,0:T(8,128)S(1)} %get-tuple-element.62), custom_call_target="InvertDiagBlocksLowerTriangular" | custom-call | tf_op jit(solution)/shard_map/jit(cholesky)/cholesky | solution.py:21
  563.9 11.7 %cholesky.147 = f32[128,128]{1,0:T(8,128)S(1)} custom-call(f32[128,128]{1,0:T(8,128)S(1)} %convolution_subtract_fusion.5), custom_call_target="Cholesky" | custom-call | tf_op jit(solution)/shard_map/jit(cholesky)/cholesky | solution.py:21
  577.6 4.0 while.2
  578.4 1.3 bitcast_dynamic-update-slice_fusion.4
  580.3 1.3 bitcast_dynamic-update-slice_fusion.4
  581.6 19.7 %custom-call.22 = f32[2,128,128]{1,2,0:T(8,128)S(1)} custom-call(f32[2,128,128]{2,1,0:T(8,128)S(1)} %get-tuple-element.11), custom_call_target="InvertDiagBlocksLowerTriangular" | custom-call | tf_op jit(solution)/shard_map/jit(_cho_solve)/triangular_solve | solution.py:22
  603.4 3.6 select_convert_fusion
  607.0 3.2 convert_bitcast_fusion
  610.3 6.8 copy.78
  617.1 10.2 %convolution_convert_fusion = bf16[256,32768]{1,0:T(8,128)(2,1)} fusion(bf16[64,32768]{1,0:T(8,128)(2,1)} %bitcast.143, s32[64]{0:T(128)S(1)} %eq.15), kind=kOutput, calls=%fused_computation.5 | convolution fusion | flops 1082146816 | bytes 20971776 | tf_op jit(solution)/shard_map/dot_general | solution.py:69
  627.3 25.6 %convert_element_type.26 = bf16[32768,256]{1,0:T(8,128)(2,1)} reshape(bf16[256,32768]{1,0:T(8,128)(2,1)} %convolution_convert_fusion) | data formatting | bytes 33554432 | tf_op jit(solution)/shard_map/convert_element_type | solution.py:71
  652.9 21.7 %copy.57 = bf16[32768,256]{0,1:T(8,128)(2,1)} copy(bf16[32768,256]{1,0:T(8,128)(2,1)} %convert_element_type.26) | data formatting | bytes 33554432 | tf_op jit(solution)/shard_map/convert_element_type | solution.py:71
  676.3 11.7 %cholesky.164 = f32[128,128]{1,0:T(8,128)S(1)} custom-call(f32[128,128]{1,0:T(8,128)S(1)} %cholesky.197), custom_call_target="Cholesky" | custom-call | tf_op jit(solution)/shard_map/jit(cholesky)/cholesky | solution.py:21
  688.0 9.8 %custom-call.26 = f32[1,128,128]{1,2,0:T(8,128)S(1)} custom-call(f32[1,128,128]{2,1,0:T(8,128)S(1)} %get-tuple-element.58), custom_call_target="InvertDiagBlocksLowerTriangular" | custom-call | tf_op jit(solution)/shard_map/jit(cholesky)/cholesky | solution.py:21
  698.4 11.7 %cholesky.181 = f32[128,128]{1,0:T(8,128)S(1)} custom-call(f32[128,128]{1,0:T(8,128)S(1)} %convolution_subtract_fusion.4), custom_call_target="Cholesky" | custom-call | tf_op jit(solution)/shard_map/jit(cholesky)/cholesky | solution.py:21
  712.7 4.0 while.3
  713.4 1.4 bitcast_dynamic-update-slice_fusion.5
  715.4 1.4 bitcast_dynamic-update-slice_fusion.5
  716.7 19.8 %custom-call.23 = f32[2,128,128]{1,2,0:T(8,128)S(1)} custom-call(f32[2,128,128]{2,1,0:T(8,128)S(1)} %get-tuple-element.19), custom_call_target="InvertDiagBlocksLowerTriangular" | custom-call | tf_op jit(solution)/shard_map/jit(_cho_solve)/triangular_solve | solution.py:22
  736.6 50.0 %reduce-scatter.5.cloned.1.call-done = bf16[2048,256]{0,1:T(8,128)(2,1)} async-done(((bf16[32768,256]{0,1:T(8,128)(2,1)}), bf16[2048,256]{0,1:T(8,128)(2,1)}) %reduce-scatter.5.cloned.1.call-update) | async-done | bytes 1048592 | tf_op jit(solution)/shard_map/reduce_scatter | solution.py:70
  786.5 1.7 fusion.8
  788.2 2.1 convolution_subtract_fusion.1
  790.3 1.0 fusion.35
  791.3 1.0 fusion.34
  792.4 1.0 convolution_subtract_fusion
  793.4 1.0 fusion.33
  794.6 1.8 copy.59
  (90 shorter events, 14.7 us)
Async XLA Ops:
  7.2 365.3 %copy-start = (f32[256,256]{1,0:T(8,128)S(1)}, f32[256,256]{1,0:T(8,128)}, u32[]{:S(2)}) copy-start(f32[256,256]{1,0:T(8,128)} %param.11) | copy-start | bytes 786436
  14.0 8.8 %copy-start.7 = (s32[16,4]{0,1:T(4,128)S(1)}, s32[16,4]{0,1:T(4,128)}, u32[]{:S(2)}) copy-start(s32[16,4]{0,1:T(4,128)} %param.8) | copy-start | bytes 772
  14.0 9.1 %copy-start.8 = (s32[16]{0:T(128)S(1)}, s32[16]{0:T(128)}, u32[]{:S(2)}) copy-start(s32[16]{0:T(128)} %param.9) | copy-start | bytes 196
  14.0 302.1 %all-to-all-start = ((bf16[16,2048,256]{2,1,0:T(8,128)(2,1)}), bf16[16,2048,256]{2,1,0:T(8,128)(2,1)}, u32[]{:S(2)}, u32[]{:S(2)}) async-start(bf16[16,2048,256]{2,1,0:T(8,128)(2,1)} %stack.2), calls=%async_computation | async-start | bytes 33554432 | tf_op jit(solution)/shard_map/all_to_all | solution.py:37
  22.8 349.6 %reduce-scatter.3.cloned.1.call-start = ((), (), s32[]{:S(2)}) async-start(), calls=%async_computation.3 | async-start | bytes 4718592 | tf_op jit(solution)/shard_map/reduce_scatter | solution.py:45
  331.4 0.7 copy-start.9
  331.4 1.9 copy-start.4
  331.4 118.4 %all-reduce.8.cloned.1.call-start = ((), (), s32[]{:S(2)}) async-start(), calls=%async_computation.7 | async-start | bytes 1572864 | tf_op jit(solution)/shard_map/psum | solution.py:52
  381.1 4.9 copy-start.3
  388.0 152.5 %all-reduce.6.cloned.1.call-start = ((), (), s32[]{:S(2)}) async-start(), calls=%async_computation.6 | async-start | bytes 1572864 | tf_op jit(solution)/shard_map/psum | solution.py:53
  449.8 153.6 %all-gather.2.cloned.1.call-start = ((), (), s32[]{:S(2)}) async-start(), calls=%async_computation.4 | async-start | bytes 2359296 | tf_op jit(solution)/shard_map/all_gather | solution.py:54
  450.4 336.2 %reduce-scatter.5.cloned.1.call-start = ((), (), s32[]{:S(2)}) async-start(), calls=%async_computation.5 | async-start | bytes 17825792 | tf_op jit(solution)/shard_map/reduce_scatter | solution.py:70
  540.5 60.8 %copy-start.6 = (f32[256,256]{0,1:T(8,128)S(1)}, f32[256,256]{0,1:T(8,128)}, u32[]{:S(2)}) copy-start(f32[256,256]{0,1:T(8,128)} %get-tuple-element.45) | copy-start | bytes 786436
  603.4 3.7 copy-start.2
  674.6 1.0 copy-start.5
  793.4 3.0 copy-start.1
Sparse Core Ops, SparseCore 0:
  331.6 40.8 reduce-scatter.2
  388.1 61.6 all-reduce.7
  453.4 87.0 all-reduce.5
  542.6 26.8 all-gather.1
  674.8 111.7 reduce-scatter.4
